TPU v7x, 32 devices: a whole 2x2x4 slice. The times are simulated.
32 devices in a mesh: snap: 2 (over y), chan: 16 (over z, x, core).
Axes of the slice: x: 2, y: 2, z: 4, core: 2. Of those that a mesh axis runs over, the one named last changes fastest.
Arguments:
- snap_tiles: bfloat16 [16, 192, 64, 128], P('snap', 'chan'), may hold values from -6 to 6
- beam_gain: float32 [16, 64, 128], P('snap'), may hold values from 0.1 to 1
- kernel: bfloat16 [16, 32, 128, 256], P(None, 'snap'), may hold values from -0.5 to 0.5
- tile_map: int32 [16, 32], replicated, may hold values from 0 to 63
- pixel_lm: float32 [2, 8192], P(None, 'snap'), may hold values from -0.5 to 0.5
- mode_uv: int32 [2, 2048], replicated, may hold values from -32 to 31
Outputs:
- sky_cube: float32 [32, 192, 256], P('snap', 'chan')
- delay_spec: float32 [2, 192, 2048], P(None, None, ('snap', 'chan'))
Inputs may be any that keep to these rules, and one draw needn't show every extreme that they name: `tile_map`: tile indices.
All inputs are finite; a program needn't handle non-finite values.
Results may differ from a plain program's by a relative error of at most 0.0047.
Values may be sent and summed in bfloat16 or wider, within the bound.
No kernel may reach another device: no remote copies, remote signals or barrier semaphores. Data moves between devices by JAX's collectives and lax.ppermute only.
A program may use at most 192 MiB of HBM per device.

v0:
```python
import math
import jax
import jax.numpy as jnp
from jax import lax
from jax.sharding import PartitionSpec as P

BLOCK_PIX = 256


def hamming(length):
    channel_index = jnp.arange(length, dtype=jnp.float32)
    return 0.54 - 0.46 * jnp.cos(channel_index * (2.0 * math.pi / (length - 1)))


def delay_transform(power_spectrum):
    length = power_spectrum.shape[1]
    channel_index = jnp.arange(length, dtype=jnp.int32)
    residues = channel_index[:, None] * channel_index[None, :] % length
    phases = residues.astype(jnp.float32) * (2.0 * math.pi / length)
    cosine = jnp.cos(phases)
    sine_part = jnp.sin(phases)
    window_gain = hamming(length)[:, None]
    real_component = power_spectrum[0] * window_gain
    imag_part = power_spectrum[1] * window_gain
    highest = lax.Precision.HIGHEST
    out_re = jnp.dot(cosine, real_component, precision=highest) + jnp.dot(
        sine_part, imag_part, precision=highest
    )
    out_im = jnp.dot(cosine, imag_part, precision=highest) - jnp.dot(
        sine_part, real_component, precision=highest
    )
    return jnp.stack([out_re, out_im]) / math.sqrt(length)


def phasor(positions, uv_grid):
    spatial = uv_grid.astype(jnp.float32)
    phase_table = (
        positions[0][:, None] * spatial[0][None, :] + positions[1][:, None] * spatial[1][None, :]
    ) * (2.0 * math.pi)
    return jnp.concatenate([jnp.cos(phase_table), -jnp.sin(phase_table)], axis=1).astype(
        jnp.bfloat16
    )


def interpolate(weighted, kernels, block_maps):
    gathered_rows = jax.vmap(
        lambda single_snapshot_tiles, one_map: jnp.take(single_snapshot_tiles, one_map, axis=1)
    )(weighted, block_maps)
    return jnp.einsum("scbt,sbtp->bcp", gathered_rows, kernels, preferred_element_type=jnp.float32)


def per_device(snap_tiles, beam_gain, kernel, tile_map, pixel_lm, mode_uv):
    snap_count = lax.axis_size("snap")
    chan_count = lax.axis_size("chan")
    snap_index = lax.axis_index("snap")
    chan_local = snap_tiles.shape[1]
    local_pixel_blocks = pixel_lm.shape[1] // BLOCK_PIX
    block_start = snap_index * local_pixel_blocks
    weighted = (snap_tiles.astype(jnp.float32) * beam_gain[:, None]).astype(jnp.bfloat16)
    own_map = lax.dynamic_slice_in_dim(tile_map, block_start, local_pixel_blocks, 1)
    sky_cube = interpolate(lax.all_gather(weighted, "snap", axis=0, tiled=True), kernel, own_map)
    cube_low = sky_cube.astype(jnp.bfloat16)
    per_group = 2
    turn_count = local_pixel_blocks // per_group
    group_width = per_group * BLOCK_PIX
    fourier_mode_count = mode_uv.shape[1]

    def add_group(turn, running):
        partial_sky_cube = lax.dynamic_slice_in_dim(cube_low, turn * per_group, per_group, 0)
        lm_part = lax.dynamic_slice_in_dim(pixel_lm, turn * group_width, group_width, 1)
        phasor_lookup = phasor(lm_part, mode_uv).reshape(
            per_group, BLOCK_PIX, 2 * fourier_mode_count
        )
        return running + jnp.einsum(
            "woj,wjh->oh", partial_sky_cube, phasor_lookup, preferred_element_type=jnp.float32
        )

    running = lax.fori_loop(
        0, turn_count, add_group, jnp.zeros((chan_local, 2 * fourier_mode_count), jnp.float32)
    )
    partial_value = running.reshape(chan_local, 2, fourier_mode_count).transpose(1, 0, 2)
    pixel_total = pixel_lm.shape[1] * snap_count
    cell_count = fourier_mode_count // (snap_count * chan_count)
    spread = partial_value.reshape(2, chan_local, snap_count, chan_count, cell_count)
    regrouped = lax.all_to_all(spread, "chan", split_axis=3, concat_axis=1, tiled=True)
    summed = lax.psum_scatter(regrouped, "snap", scatter_dimension=2, tiled=True)
    scaled = summed.reshape(2, chan_local * chan_count, cell_count) / math.sqrt(pixel_total)
    delay_spec = delay_transform(scaled)
    return (sky_cube, delay_spec)


def solution(mesh):
    return jax.shard_map(
        per_device,
        mesh=mesh,
        in_specs=(
            P("snap", "chan", None, None),
            P("snap", None, None),
            P(None, "snap", None, None),
            P(),
            P(None, "snap"),
            P(),
        ),
        out_specs=(P("snap", "chan", None), P(None, None, ("snap", "chan"))),
        check_vma=False,
    )
```

profile of v0, /device:TPU:0, one launch (start us, length us, event | category | flops | bytes accessed | tf_op | source)
XLA Modules:
  0.0 277.3 jit_solution(12588027699825546951)
XLA Ops:
  7.2 3.1 %multiply_convert_fusion = bf16[8,12,64,128]{3,2,1,0:T(8,128)(2,1)} fusion(bf16[8,12,64,128]{3,2,1,0:T(8,128)(2,1)} %param.8, f32[8,64,128]{2,1,0:T(8,128)} %param.9), kind=kLoop, calls=%fused_computation.16 | loop fusion | flops 2359296 | bytes 3407872 | tf_op jit(solution)/shard_map/convert_element_type | solution.py:59
  10.8 47.4 %all-gather.2.cloned.1.call-done = bf16[16,12,64,128]{3,2,1,0:T(8,128)(2,1)} async-done(((bf16[8,12,64,128]{3,2,1,0:T(8,128)(2,1)}), bf16[16,12,64,128]{3,2,1,0:T(8,128)(2,1)}) %all-gather.2.cloned.1.call-update) | async-done | bytes 3145744 | tf_op jit(solution)/shard_map/all_gather | solution.py:61
  58.2 6.5 %copy.27 = bf16[16,12,64,128]{3,1,2,0:T(8,128)(2,1)} copy(bf16[16,12,64,128]{3,2,1,0:T(8,128)(2,1)} %all-gather.2.cloned.1.call-done) | data formatting | bytes 6291456 | tf_op jit(solution)/shard_map/all_gather | solution.py:61
  64.6 3.4 %gather_fusion = bf16[256,12,128]{2,1,0:T(8,128)(2,1)S(1)} fusion(bf16[16,12,64,128]{3,1,2,0:T(8,128)(2,1)} %copy.27, s32[256]{0:T(256)S(1)} %reshape.93), kind=kCustom, calls=%fused_computation | custom fusion | bytes 1574912 | tf_op jit(solution)/shard_map/vmap(jit(_take))/gather | solution.py:47
  68.1 7.0 %fusion.67 = (bf16[16,12,256]{2,1,0:T(8,128)(2,1)S(1)}, f32[16,12,256]{2,1,0:T(8,128)S(1)}) fusion(bf16[16,16,128,256]{3,2,1,0:T(8,128)(2,1)} %param.10, bf16[16,16,12,128]{3,2,1,0:T(8,128)(2,1)S(1)} %bitcast.60, pred[16,16]{0,1:T(8,128)(4,1)S(1)} %copy.26), kind=kOutput, calls=%fused_computation.74 | convolution fusion | flops 201768960 | bytes 17858816 | tf_op jit(solution)/shard_map/scbt,sbtp->bcp/dot_general | solution.py:49
  75.1 162.2 %while.16 = (s32[]{:T(128)}, f32[12,4096]{1,0:T(8,128)S(1)}, bf16[16,12,256]{2,1,0:T(8,128)(2,1)S(1)}, f32[2,4096]{1,0:T(2,128)}, f32[2,2048]{1,0:T(2,128)S(1)},...) while((s32[]{:T(128)}, f32[12,4096]{1,0:T(8,128)S(1)}, ...), condition=%wide.region_1.2_spmd.clone, body=%wide.region_0.1_spmd.clone.sunk | while | flops 66158604 | bytes 8933627 | solution.py:78
  76.0 17.1 %cosine_convert_fusion.2 = (bf16[2,256,2048]{2,1,0:T(8,128)(2,1)S(1)}, bf16[2,256,2048]{2,1,0:T(8,128)(2,1)}) fusion(f32[2048]{0:T(1024)S(1)} %bitcast.58, f32[2,256]{1,0:T(2,128)S(1)} %mul.440, f32[2048]{0:T(1024)S(1)} %bitcast.57, f32[2,256]{1,0:T(2,128)S(1)} %mul.441), kind=kLoop, calls=%fused_computation.7.clone.1 | loop fusion | flops 7340032 | bytes 4214784 | tf_op jit(solution)/shard_map/convert
  93.1 2.2 fusion.75
  96.3 17.1 %cosine_convert_fusion.2 = (bf16[2,256,2048]{2,1,0:T(8,128)(2,1)S(1)}, bf16[2,256,2048]{2,1,0:T(8,128)(2,1)}) fusion(f32[2048]{0:T(1024)S(1)} %bitcast.58, f32[2,256]{1,0:T(2,128)S(1)} %mul.440, f32[2048]{0:T(1024)S(1)} %bitcast.57, f32[2,256]{1,0:T(2,128)S(1)} %mul.441), kind=kLoop, calls=%fused_computation.7.clone.1 | loop fusion | flops 7340032 | bytes 4214784 | tf_op jit(solution)/shard_map/convert
  113.4 2.2 fusion.75
  116.5 17.1 %cosine_convert_fusion.2 = (bf16[2,256,2048]{2,1,0:T(8,128)(2,1)S(1)}, bf16[2,256,2048]{2,1,0:T(8,128)(2,1)}) fusion(f32[2048]{0:T(1024)S(1)} %bitcast.58, f32[2,256]{1,0:T(2,128)S(1)} %mul.440, f32[2048]{0:T(1024)S(1)} %bitcast.57, f32[2,256]{1,0:T(2,128)S(1)} %mul.441), kind=kLoop, calls=%fused_computation.7.clone.1 | loop fusion | flops 7340032 | bytes 4214784 | tf_op jit(solution)/shard_map/convert
  133.6 2.2 fusion.75
  136.8 17.1 %cosine_convert_fusion.2 = (bf16[2,256,2048]{2,1,0:T(8,128)(2,1)S(1)}, bf16[2,256,2048]{2,1,0:T(8,128)(2,1)}) fusion(f32[2048]{0:T(1024)S(1)} %bitcast.58, f32[2,256]{1,0:T(2,128)S(1)} %mul.440, f32[2048]{0:T(1024)S(1)} %bitcast.57, f32[2,256]{1,0:T(2,128)S(1)} %mul.441), kind=kLoop, calls=%fused_computation.7.clone.1 | loop fusion | flops 7340032 | bytes 4214784 | tf_op jit(solution)/shard_map/convert
  153.9 2.2 fusion.75
  157.1 17.1 %cosine_convert_fusion.2 = (bf16[2,256,2048]{2,1,0:T(8,128)(2,1)S(1)}, bf16[2,256,2048]{2,1,0:T(8,128)(2,1)}) fusion(f32[2048]{0:T(1024)S(1)} %bitcast.58, f32[2,256]{1,0:T(2,128)S(1)} %mul.440, f32[2048]{0:T(1024)S(1)} %bitcast.57, f32[2,256]{1,0:T(2,128)S(1)} %mul.441), kind=kLoop, calls=%fused_computation.7.clone.1 | loop fusion | flops 7340032 | bytes 4214784 | tf_op jit(solution)/shard_map/convert
  174.2 2.2 fusion.75
  177.4 17.1 %cosine_convert_fusion.2 = (bf16[2,256,2048]{2,1,0:T(8,128)(2,1)S(1)}, bf16[2,256,2048]{2,1,0:T(8,128)(2,1)}) fusion(f32[2048]{0:T(1024)S(1)} %bitcast.58, f32[2,256]{1,0:T(2,128)S(1)} %mul.440, f32[2048]{0:T(1024)S(1)} %bitcast.57, f32[2,256]{1,0:T(2,128)S(1)} %mul.441), kind=kLoop, calls=%fused_computation.7.clone.1 | loop fusion | flops 7340032 | bytes 4214784 | tf_op jit(solution)/shard_map/convert
  194.5 2.2 fusion.75
  197.6 17.1 %cosine_convert_fusion.2 = (bf16[2,256,2048]{2,1,0:T(8,128)(2,1)S(1)}, bf16[2,256,2048]{2,1,0:T(8,128)(2,1)}) fusion(f32[2048]{0:T(1024)S(1)} %bitcast.58, f32[2,256]{1,0:T(2,128)S(1)} %mul.440, f32[2048]{0:T(1024)S(1)} %bitcast.57, f32[2,256]{1,0:T(2,128)S(1)} %mul.441), kind=kLoop, calls=%fused_computation.7.clone.1 | loop fusion | flops 7340032 | bytes 4214784 | tf_op jit(solution)/shard_map/convert
  214.7 2.2 fusion.75
  217.9 17.1 %cosine_convert_fusion.2 = (bf16[2,256,2048]{2,1,0:T(8,128)(2,1)S(1)}, bf16[2,256,2048]{2,1,0:T(8,128)(2,1)}) fusion(f32[2048]{0:T(1024)S(1)} %bitcast.58, f32[2,256]{1,0:T(2,128)S(1)} %mul.440, f32[2048]{0:T(1024)S(1)} %bitcast.57, f32[2,256]{1,0:T(2,128)S(1)} %mul.441), kind=kLoop, calls=%fused_computation.7.clone.1 | loop fusion | flops 7340032 | bytes 4214784 | tf_op jit(solution)/shard_map/convert
  235.0 2.2 fusion.75
  238.3 14.4 %all_to_all.18 = f32[16,1,3072]{2,1,0:T(1,128)S(1)} all-to-all(f32[16,1,3072]{2,1,0:T(1,128)S(1)} %reshape.118), channel_id=1, replica_groups=mesh['snap'=2,'chan'=16] {'chan'}, dimensions={0} | all-to-all | bytes 393216 | tf_op jit(solution)/shard_map/all_to_all | solution.py:85
  256.5 8.1 %reduce-scatter.2.cloned.1.call-done = f32[2,192,1,1,64]{1,4,3,0,2:T(8,128)} async-done(((f32[2,192,2,1,64]{1,4,3,0,2:T(8,128)}), f32[2,192,1,1,64]{1,4,3,0,2:T(8,128)}) %reduce-scatter.2.cloned.1.call-update) | async-done | bytes 98320 | tf_op jit(solution)/shard_map/reduce_scatter | solution.py:86
  (62 shorter events, 18.4 us)
Async XLA Ops:
  7.2 3.3 %copy-start = (s32[16,32]{1,0:T(8,128)S(1)}, s32[16,32]{1,0:T(8,128)}, u32[]{:S(2)}) copy-start(s32[16,32]{1,0:T(8,128)} %param.11) | copy-start | bytes 6148
  7.2 3.6 %copy-start.1 = (s32[2,2048]{1,0:T(2,128)S(1)}, s32[2,2048]{1,0:T(2,128)}, u32[]{:S(2)}) copy-start(s32[2,2048]{1,0:T(2,128)} %param.13) | copy-start | bytes 49156
  7.2 51.0 %all-gather.2.cloned.1.call-start = ((), (), s32[]{:S(2)}) async-start(), calls=%async_computation.2 | async-start | bytes 4718592 | tf_op jit(solution)/shard_map/all_gather | solution.py:61
  10.4 254.1 %reduce-scatter.2.cloned.1.call-start = ((), (), s32[]{:S(2)}) async-start(), calls=%async_computation.3 | async-start | bytes 393216 | tf_op jit(solution)/shard_map/reduce_scatter | solution.py:86
Sparse Core Ops, SparseCore 0:
  10.5 47.6 all-gather.1
  255.7 8.7 reduce-scatter.1
where the time goes:
time: 278 us; the launch traced here: 277 us
  other arithmetic  143 us (51%)
  waiting for transfers between devices  55.4 us (20%)
  matrix products  29.4 us (11%)
  local copies, waits for them, and re-layouts  20.9 us (8%)
  blocking collectives  14.4 us (5%)
  between operations  14.1 us (5%)
    another operation x8, other arithmetic  137 us
    all_gather x1, waiting for transfers between devices, per_device(): lax.all_gather(weighted, 'snap', axis=0, tiled=True)  47.4 us
    dot_general x8, matrix products, add_group(): jnp.einsum('woj,wjh->oh', partial_sky_cube, phasor_lookup, preferred_elem...  18 us
    all_to_all x1, blocking collectives, per_device(): lax.all_to_all(spread, 'chan', split_axis=3, concat_axis=1, tiled=True)  14.4 us
    reduce_scatter x1, waiting for transfers between devices, per_device(): lax.psum_scatter(regrouped, 'snap', scatter_dimension=2, tiled=True)  8.05 us
    dot_general x1, matrix products, interpolate(): jnp.einsum('scbt,sbtp->bcp', gathered_rows, kernels, preferred_element_ty...  7.02 us
    slice x8, local copies, waits for them, and re-layouts, phasor(): positions[0][:, None] * spatial[0][None, :]  6.85 us
    all_gather x1, local copies, waits for them, and re-layouts, per_device(): lax.all_gather(weighted, 'snap', axis=0, tiled=True)  6.46 us
  transfers between devices with their start and end apart: 2, of which 2 were waited for; matrix products, arithmetic and copies ran while one was open for 0% of the time, Pallas kernels for 0%

commit v1 on v0

--- a/solution.py
+++ b/solution.py
@@ -5,6 +5,18 @@
 from jax.sharding import PartitionSpec as P
 
 BLOCK_PIX = 256
+
+
+def collect(x, axis, dim):
+    ways, here, lap = (lax.axis_size(axis), lax.axis_index(axis), x.shape[dim])
+    line, have = (x, 1)
+    while have < ways:
+        line = jnp.concatenate(
+            [line, lax.ppermute(line, axis, [(d, (d - have) % ways) for d in range(ways)])],
+            axis=dim,
+        )
+        have = 2 * have
+    return jnp.roll(line, here * lap, axis=dim)
 
 
 def hamming(length):
@@ -58,7 +70,7 @@
     block_start = snap_index * local_pixel_blocks
     weighted = (snap_tiles.astype(jnp.float32) * beam_gain[:, None]).astype(jnp.bfloat16)
     own_map = lax.dynamic_slice_in_dim(tile_map, block_start, local_pixel_blocks, 1)
-    sky_cube = interpolate(lax.all_gather(weighted, "snap", axis=0, tiled=True), kernel, own_map)
+    sky_cube = interpolate(collect(weighted, "snap", 0), kernel, own_map)
     cube_low = sky_cube.astype(jnp.bfloat16)
     per_group = 2
     turn_count = local_pixel_blocks // per_group

time: 278 us -> 269 us (0.968)
  waiting for transfers between devices: 55.4 us -> 41 us
  starting transfers between devices: 0.08 us -> 3.1 us
  other arithmetic: 143 us -> 146 us
    all_gather x1 -> x0, waiting for transfers between devices: 47.4 us -> none  [per_device(): lax.all_gather(weighted, 'snap', axis=0, tiled=True)]
    ppermute x0 -> x1, waiting for transfers between devices: none -> 31.9 us  [collect(): lax.ppermute(line, axis, [(d, (d - have) % ways) for d in range(ways)])]
    all_gather x1 -> x0, local copies, waits for them, and re-layouts: 6.46 us -> none  [per_device(): lax.all_gather(weighted, 'snap', axis=0, tiled=True)]
    dynamic_slice x0 -> x1, local copies, waits for them, and re-layouts: none -> 4.58 us  [collect(): return jnp.roll(line, here * lap, axis=dim)]
    ppermute x0 -> x1, starting transfers between devices: none -> 3.06 us  [collect(): lax.ppermute(line, axis, [(d, (d - have) % ways) for d in range(ways)])]
  transfers between devices with their start and end apart: 2 -> 2, of which waited for: 2 -> 2; matrix products, arithmetic and copies ran while one was open for 0% -> 1% of each run, Pallas kernels for 0% -> 0%
where the time goes in v1:
time: 269 us; the launch traced here: 268 us
  other arithmetic  146 us (54%)
  waiting for transfers between devices  41 us (15%)
  matrix products  29.4 us (11%)
  local copies, waits for them, and re-layouts  19 us (7%)
  blocking collectives  14.9 us (6%)
  between operations  14.1 us (5%)
  starting transfers between devices  3.1 us (1%)
    another operation x8, other arithmetic  137 us
    ppermute x1, waiting for transfers between devices, collect(): lax.ppermute(line, axis, [(d, (d - have) % ways) for d in range(ways)])  31.9 us
    dot_general x8, matrix products, add_group(): jnp.einsum('woj,wjh->oh', partial_sky_cube, phasor_lookup, preferred_elem...  18 us
    all_to_all x1, blocking collectives, per_device(): lax.all_to_all(spread, 'chan', split_axis=3, concat_axis=1, tiled=True)  14.9 us
    reduce_scatter x1, waiting for transfers between devices, per_device(): lax.psum_scatter(regrouped, 'snap', scatter_dimension=2, tiled=True)  9.01 us
    dot_general x1, matrix products, interpolate(): jnp.einsum('scbt,sbtp->bcp', gathered_rows, kernels, preferred_element_ty...  7.02 us
    slice x8, local copies, waits for them, and re-layouts, phasor(): positions[0][:, None] * spatial[0][None, :]  6.87 us
  transfers between devices with their start and end apart: 2, of which 2 were waited for; matrix products, arithmetic and copies ran while one was open for 1% of the time, Pallas kernels for 0%

profile of v1, /device:TPU:0, one launch (start us, length us, event | category | flops | bytes accessed | tf_op | source)
XLA Modules:
  0.0 267.8 jit_solution(1228303697575822609)
XLA Ops:
  9.1 3.1 %collective-permute-start = (bf16[8,12,64,128]{3,2,1,0:T(8,128)(2,1)S(1)}, bf16[8,12,64,128]{3,2,1,0:T(8,128)(2,1)S(1)}, u32[]{:S(2)}, u32[]{:S(2)}) collective-permute-start(bf16[8,12,64,128]{3,2,1,0:T(8,128)(2,1)S(1)} %multiply_convert_fusion), channel_id=1, source_target_pairs={{0,16},{16,0},{1,17},{17,1},{2,18},{18,2},{3,19},{19,3},{4,20},{20... | collective-permute-start | bytes 4718600 | tf_op jit(solution)/shard_map/ppermute | solution.py:15
  14.7 31.9 %collective-permute-done = bf16[8,12,64,128]{3,2,1,0:T(8,128)(2,1)S(1)} collective-permute-done((bf16[8,12,64,128]{3,2,1,0:T(8,128)(2,1)S(1)}, bf16[8,12,64,128]{3,2,1,0:T(8,128)(2,1)S(1)}, u32[]{:S(2)}, u32[]{:S(2)}) %collective-permute-start) | collective-permute-done | bytes 1572896 | tf_op jit(solution)/shard_map/ppermute | solution.py:15
  48.8 4.6 %copy.39 = bf16[16,12,64,128]{3,1,2,0:T(8,128)(2,1)} copy(bf16[16,12,64,128]{3,2,1,0:T(8,128)(2,1)S(1)} %fusion.11) | data formatting | bytes 6291456 | tf_op jit(solution)/shard_map/jit(_roll_dynamic)/dynamic_slice | solution.py:19
  53.3 3.4 %gather_fusion = bf16[256,12,128]{2,1,0:T(8,128)(2,1)S(1)} fusion(bf16[16,12,64,128]{3,1,2,0:T(8,128)(2,1)} %copy.39, s32[256]{0:T(256)S(1)} %reshape.93), kind=kCustom, calls=%fused_computation | custom fusion | bytes 1574912 | tf_op jit(solution)/shard_map/vmap(jit(_take))/gather | solution.py:59
  56.8 7.0 %fusion.70 = (bf16[16,12,256]{2,1,0:T(8,128)(2,1)S(1)}, f32[16,12,256]{2,1,0:T(8,128)S(1)}) fusion(bf16[16,16,128,256]{3,2,1,0:T(8,128)(2,1)} %param.10, bf16[16,16,12,128]{3,2,1,0:T(8,128)(2,1)S(1)} %bitcast.60, pred[16,16]{0,1:T(8,128)(4,1)S(1)} %copy.38), kind=kOutput, calls=%fused_computation.81 | convolution fusion | flops 201768960 | bytes 17858816 | tf_op jit(solution)/shard_map/scbt,sbtp->bcp/dot_general | solution.py:61
  63.8 162.4 %while.16 = (s32[]{:T(128)}, f32[12,4096]{1,0:T(8,128)S(1)}, bf16[16,12,256]{2,1,0:T(8,128)(2,1)S(1)}, f32[2,4096]{1,0:T(2,128)}, f32[2,2048]{1,0:T(2,128)S(1)},...) while((s32[]{:T(128)}, f32[12,4096]{1,0:T(8,128)S(1)}, ...), condition=%wide.region_1.2_spmd.clone, body=%wide.region_0.1_spmd.clone.sunk | while | flops 66158604 | bytes 8933619 | solution.py:90
  64.7 17.1 %cosine_convert_fusion.2 = (bf16[2,256,2048]{2,1,0:T(8,128)(2,1)S(1)}, bf16[2,256,2048]{2,1,0:T(8,128)(2,1)}) fusion(f32[2048]{0:T(1024)S(1)} %bitcast.58, f32[2,256]{1,0:T(2,128)S(1)} %mul.444, f32[2048]{0:T(1024)S(1)} %bitcast.57, f32[2,256]{1,0:T(2,128)S(1)} %mul.445), kind=kLoop, calls=%fused_computation.7.clone.1 | loop fusion | flops 7340032 | bytes 4214784 | tf_op jit(solution)/shard_map/convert
  81.8 2.3 fusion.78
  85.0 17.1 %cosine_convert_fusion.2 = (bf16[2,256,2048]{2,1,0:T(8,128)(2,1)S(1)}, bf16[2,256,2048]{2,1,0:T(8,128)(2,1)}) fusion(f32[2048]{0:T(1024)S(1)} %bitcast.58, f32[2,256]{1,0:T(2,128)S(1)} %mul.444, f32[2048]{0:T(1024)S(1)} %bitcast.57, f32[2,256]{1,0:T(2,128)S(1)} %mul.445), kind=kLoop, calls=%fused_computation.7.clone.1 | loop fusion | flops 7340032 | bytes 4214784 | tf_op jit(solution)/shard_map/convert
  102.1 2.3 fusion.78
  105.3 17.1 %cosine_convert_fusion.2 = (bf16[2,256,2048]{2,1,0:T(8,128)(2,1)S(1)}, bf16[2,256,2048]{2,1,0:T(8,128)(2,1)}) fusion(f32[2048]{0:T(1024)S(1)} %bitcast.58, f32[2,256]{1,0:T(2,128)S(1)} %mul.444, f32[2048]{0:T(1024)S(1)} %bitcast.57, f32[2,256]{1,0:T(2,128)S(1)} %mul.445), kind=kLoop, calls=%fused_computation.7.clone.1 | loop fusion | flops 7340032 | bytes 4214784 | tf_op jit(solution)/shard_map/convert
  122.4 2.3 fusion.78
  125.6 17.1 %cosine_convert_fusion.2 = (bf16[2,256,2048]{2,1,0:T(8,128)(2,1)S(1)}, bf16[2,256,2048]{2,1,0:T(8,128)(2,1)}) fusion(f32[2048]{0:T(1024)S(1)} %bitcast.58, f32[2,256]{1,0:T(2,128)S(1)} %mul.444, f32[2048]{0:T(1024)S(1)} %bitcast.57, f32[2,256]{1,0:T(2,128)S(1)} %mul.445), kind=kLoop, calls=%fused_computation.7.clone.1 | loop fusion | flops 7340032 | bytes 4214784 | tf_op jit(solution)/shard_map/convert
  142.7 2.3 fusion.78
  145.9 17.1 %cosine_convert_fusion.2 = (bf16[2,256,2048]{2,1,0:T(8,128)(2,1)S(1)}, bf16[2,256,2048]{2,1,0:T(8,128)(2,1)}) fusion(f32[2048]{0:T(1024)S(1)} %bitcast.58, f32[2,256]{1,0:T(2,128)S(1)} %mul.444, f32[2048]{0:T(1024)S(1)} %bitcast.57, f32[2,256]{1,0:T(2,128)S(1)} %mul.445), kind=kLoop, calls=%fused_computation.7.clone.1 | loop fusion | flops 7340032 | bytes 4214784 | tf_op jit(solution)/shard_map/convert
  163.1 2.3 fusion.78
  166.2 17.1 %cosine_convert_fusion.2 = (bf16[2,256,2048]{2,1,0:T(8,128)(2,1)S(1)}, bf16[2,256,2048]{2,1,0:T(8,128)(2,1)}) fusion(f32[2048]{0:T(1024)S(1)} %bitcast.58, f32[2,256]{1,0:T(2,128)S(1)} %mul.444, f32[2048]{0:T(1024)S(1)} %bitcast.57, f32[2,256]{1,0:T(2,128)S(1)} %mul.445), kind=kLoop, calls=%fused_computation.7.clone.1 | loop fusion | flops 7340032 | bytes 4214784 | tf_op jit(solution)/shard_map/convert
  183.4 2.3 fusion.78
  186.5 17.1 %cosine_convert_fusion.2 = (bf16[2,256,2048]{2,1,0:T(8,128)(2,1)S(1)}, bf16[2,256,2048]{2,1,0:T(8,128)(2,1)}) fusion(f32[2048]{0:T(1024)S(1)} %bitcast.58, f32[2,256]{1,0:T(2,128)S(1)} %mul.444, f32[2048]{0:T(1024)S(1)} %bitcast.57, f32[2,256]{1,0:T(2,128)S(1)} %mul.445), kind=kLoop, calls=%fused_computation.7.clone.1 | loop fusion | flops 7340032 | bytes 4214784 | tf_op jit(solution)/shard_map/convert
  203.7 2.3 fusion.78
  206.8 17.1 %cosine_convert_fusion.2 = (bf16[2,256,2048]{2,1,0:T(8,128)(2,1)S(1)}, bf16[2,256,2048]{2,1,0:T(8,128)(2,1)}) fusion(f32[2048]{0:T(1024)S(1)} %bitcast.58, f32[2,256]{1,0:T(2,128)S(1)} %mul.444, f32[2048]{0:T(1024)S(1)} %bitcast.57, f32[2,256]{1,0:T(2,128)S(1)} %mul.445), kind=kLoop, calls=%fused_computation.7.clone.1 | loop fusion | flops 7340032 | bytes 4214784 | tf_op jit(solution)/shard_map/convert
  224.0 2.3 fusion.78
  227.3 14.9 %all_to_all.18 = f32[16,1,3072]{2,1,0:T(1,128)S(1)} all-to-all(f32[16,1,3072]{2,1,0:T(1,128)S(1)} %reshape.118), channel_id=1, replica_groups=mesh['snap'=2,'chan'=16] {'chan'}, dimensions={0} | all-to-all | bytes 393216 | tf_op jit(solution)/shard_map/all_to_all | solution.py:97
  246.0 9.0 %reduce-scatter.2.cloned.1.call-done = f32[2,192,1,1,64]{1,4,3,0,2:T(8,128)} async-done(((f32[2,192,2,1,64]{1,4,3,0,2:T(8,128)}), f32[2,192,1,1,64]{1,4,3,0,2:T(8,128)}) %reduce-scatter.2.cloned.1.call-update) | async-done | bytes 98320 | tf_op jit(solution)/shard_map/reduce_scatter | solution.py:98
  (58 shorter events, 24.5 us)
Async XLA Ops:
  7.2 247.8 %reduce-scatter.2.cloned.1.call-start = ((), (), s32[]{:S(2)}) async-start(), calls=%async_computation.2 | async-start | bytes 393216 | tf_op jit(solution)/shard_map/reduce_scatter | solution.py:98
  9.1 37.5 %collective-permute-start = (bf16[8,12,64,128]{3,2,1,0:T(8,128)(2,1)S(1)}, bf16[8,12,64,128]{3,2,1,0:T(8,128)(2,1)S(1)}, u32[]{:S(2)}, u32[]{:S(2)}) collective-permute-start(bf16[8,12,64,128]{3,2,1,0:T(8,128)(2,1)S(1)} %multiply_convert_fusion), channel_id=1, source_target_pairs={{0,16},{16,0},{1,17},{17,1},{2,18},{18,2},{3,19},{19,3},{4,20},{20... | collective-permute-start | bytes 4718600 | tf_op jit(solution)/shard_map/ppermute | solution.py:15
Sparse Core Ops, SparseCore 0:
  245.2 9.6 reduce-scatter.1
